TPU v7x, 32 devices: a whole 2x2x4 slice. The times are simulated.
32 devices in a mesh: section: 4 (over x, core), row: 4 (over z), col: 2 (over y).
Axes of the slice: x: 2, y: 2, z: 4, core: 2. Of those that a mesh axis runs over, the one named last changes fastest.
Arguments:
- frames: bfloat16 [3, 64, 64, 128], P(None, 'row', 'col'), may hold values from -6 to 6
- gate_weight: bfloat16 [4, 9, 256, 512], P('section'), may hold values from -0.16666667 to 0.16666667
- gate_bias: float32 [4, 512], P('section'), may hold values from -4 to 4
Outputs:
- hidden_final: bfloat16 [4, 64, 64, 128], P('section', 'row', 'col')
- cell_final: float32 [4, 64, 64, 128], P('section', 'row', 'col')
All inputs are finite; a program needn't handle non-finite values.
Results may differ from a plain program's by a relative error of at most 0.0033.
Values may be sent and summed in bfloat16 or wider, within the bound.
A program may use at most 64 MiB of HBM per device.

v0:
```python
import jax
import jax.numpy as jnp
from jax import lax
from jax.sharding import PartitionSpec as P


def with_halo(cells, sides, width):
    for axis, dim in sides:
        count = lax.axis_size(axis)
        ends = count - 1
        head = lax.slice_in_dim(cells, 0, width, axis=dim)
        tail = lax.slice_in_dim(cells, cells.shape[dim] - width, cells.shape[dim], axis=dim)
        cells = jnp.concatenate(
            [
                lax.ppermute(tail, axis, [(i, (i + 1) % count) for i in range(ends)]),
                cells,
                lax.ppermute(head, axis, [((i + 1) % count, i) for i in range(ends)]),
            ],
            axis=dim,
        )
    return cells


def passed_along(value, axis, steps):
    count = lax.axis_size(axis)
    initial, last = (max(0, -steps), min(count, count - steps))
    return lax.ppermute(value, axis, [(source, source + steps) for source in range(initial, last)])


def extend(field):
    return with_halo(field, (("row", 0), ("col", 1)), 1)


def patches(padded, rows, cols):
    pieces = [
        padded[offset // 3 : offset // 3 + rows, offset % 3 : offset % 3 + cols]
        for offset in range(9)
    ]
    return jnp.concatenate(pieces, axis=-1).reshape(rows * cols, -1)


def shards(frames, gate_weight, gate_bias):
    steps_in = frames.shape[0]
    rows, cols, width = (frames.shape[1], frames.shape[2], frames.shape[3])
    section_pos = lax.axis_index("section")
    kernel = gate_weight[0]
    stacked_kernel = kernel.reshape(9 * 2 * width, 4 * width)
    bias = gate_bias[0]
    hidden = jnp.zeros((rows, cols, width), jnp.bfloat16)
    cell = jnp.zeros((rows, cols, width), jnp.float32)
    for clock in range(steps_in + lax.axis_size("section") - 1):
        incoming = passed_along(hidden, "section", 1)
        layer_input = jnp.where(section_pos == 0, frames[min(clock, steps_in - 1)], incoming)
        padded = extend(jnp.concatenate([layer_input, hidden], axis=-1))
        pre = jnp.dot(
            patches(padded, rows, cols), stacked_kernel, preferred_element_type=jnp.float32
        )
        pre = (pre + bias).reshape(rows, cols, 4 * width)
        gate_in = pre[..., :width]
        forget = pre[..., width : 2 * width]
        candidate = pre[..., 2 * width : 3 * width]
        gate_out = pre[..., 3 * width :]
        new_cell = jax.nn.sigmoid(forget) * cell + jax.nn.sigmoid(gate_in) * jnp.tanh(candidate)
        new_hidden = (jax.nn.sigmoid(gate_out) * jnp.tanh(new_cell)).astype(jnp.bfloat16)
        active = jnp.logical_and(clock - section_pos >= 0, clock - section_pos < steps_in)
        cell = jnp.where(active, new_cell, cell)
        hidden = jnp.where(active, new_hidden, hidden)
    return (hidden[None], cell[None])


def solution(mesh):
    return jax.shard_map(
        shards,
        mesh=mesh,
        in_specs=(P(None, "row", "col", None), P("section", None, None, None), P("section", None)),
        out_specs=(P("section", "row", "col", None), P("section", "row", "col", None)),
        check_vma=False,
    )
```

profile of v0, /device:TPU:2, one launch (start us, length us, event | category | flops | bytes accessed | tf_op | source)
XLA Modules:
  0.0 156.6 jit_solution(3752703543890029598)
XLA Ops:
  0.7 2.1 %collective-permute-start = (bf16[16,32,128]{2,1,0:T(8,128)(2,1)S(1)}, bf16[16,32,128]{2,1,0:T(8,128)(2,1)S(1)}, u32[]{:S(2)}, u32[]{:S(2)}) collective-permute-start(bf16[16,32,128]{2,1,0:T(8,128)(2,1)S(1)} %broadcast_in_dim.12), channel_id=1, source_target_pairs={{0,8},{8,16},{16,24},{1,9},{9,17},{17,25},{2,10},{10,18},{18,26},{... | collective-permute-start | bytes 393224 | tf_op jit(solution)/shard_map/ppermute | solution.py:27
  2.7 4.4 %collective-permute-done = bf16[16,32,128]{2,1,0:T(8,128)(2,1)S(1)} collective-permute-done((bf16[16,32,128]{2,1,0:T(8,128)(2,1)S(1)}, bf16[16,32,128]{2,1,0:T(8,128)(2,1)S(1)}, u32[]{:S(2)}, u32[]{:S(2)}) %collective-permute-start) | collective-permute-done | bytes 131104 | tf_op jit(solution)/shard_map/ppermute | solution.py:27
  7.1 0.9 bitcast_select_fusion
  8.0 3.5 %collective-permute-start.1 = (bf16[1,32,256]{2,1,0:T(8,128)(2,1)S(1)}, bf16[1,32,256]{2,1,0:T(8,128)(2,1)S(1)}, u32[]{:S(2)}, u32[]{:S(2)}) collective-permute-start(bf16[1,32,256]{2,1,0:T(8,128)(2,1)S(1)} %get-tuple-element.50), channel_id=1, source_target_pairs={{0,2},{2,4},{4,6},{1,3},{3,5},{5,7},{8,10},{10,12},{12,14},{9,11},... | collective-permute-start | bytes 49160 | tf_op jit(solution)/shard_map/ppermute | solution.py:15
  11.5 1.3 collective-permute-start.2
  12.9 4.2 %collective-permute-done.2 = bf16[1,32,256]{2,1,0:T(8,128)(2,1)S(1)} collective-permute-done((bf16[1,32,256]{2,1,0:T(8,128)(2,1)S(1)}, bf16[1,32,256]{2,1,0:T(8,128)(2,1)S(1)}, u32[]{:S(2)}, u32[]{:S(2)}) %collective-permute-start.2) | collective-permute-done | bytes 16416 | tf_op jit(solution)/shard_map/ppermute | solution.py:17
  17.2 3.4 %collective-permute-start.3 = (bf16[18,1,256]{2,1,0:T(2,128)(2,1)S(1)}, bf16[18,1,256]{2,1,0:T(2,128)(2,1)S(1)}, u32[]{:S(2)}, u32[]{:S(2)}) collective-permute-start(bf16[18,1,256]{2,1,0:T(2,128)(2,1)S(1)} %get-tuple-element.39), channel_id=1, source_target_pairs={{0,1},{2,3},{4,5},{6,7},{8,9},{10,11},{12,13},{14,15},{16,17},{18,... | collective-permute-start | bytes 27656 | tf_op jit(solution)/shard_map/ppermute | solution.py:15
  20.6 1.3 collective-permute-start.4
  22.1 4.2 %collective-permute-done.4 = bf16[18,1,256]{2,1,0:T(2,128)(2,1)S(1)} collective-permute-done((bf16[18,1,256]{2,1,0:T(2,128)(2,1)S(1)}, bf16[18,1,256]{2,1,0:T(2,128)(2,1)S(1)}, u32[]{:S(2)}, u32[]{:S(2)}) %collective-permute-start.4) | collective-permute-done | bytes 9248 | tf_op jit(solution)/shard_map/ppermute | solution.py:17
  27.2 1.4 convolution_add_fusion.5
  28.8 1.9 %collective-permute-start.5 = (bf16[16,32,128]{2,1,0:T(8,128)(2,1)S(1)}, bf16[16,32,128]{2,1,0:T(8,128)(2,1)S(1)}, u32[]{:S(2)}, u32[]{:S(2)}) collective-permute-start(bf16[16,32,128]{2,1,0:T(8,128)(2,1)S(1)} %get-tuple-element.14), channel_id=1, source_target_pairs={{0,8},{8,16},{16,24},{1,9},{9,17},{17,25},{2,10},{10,18},{18,26},{... | collective-permute-start | bytes 393224 | tf_op jit(solution)/shard_map/ppermute | solution.py:27
  30.8 4.4 %collective-permute-done.5 = bf16[16,32,128]{2,1,0:T(8,128)(2,1)S(1)} collective-permute-done((bf16[16,32,128]{2,1,0:T(8,128)(2,1)S(1)}, bf16[16,32,128]{2,1,0:T(8,128)(2,1)S(1)}, u32[]{:S(2)}, u32[]{:S(2)}) %collective-permute-start.5) | collective-permute-done | bytes 131104 | tf_op jit(solution)/shard_map/ppermute | solution.py:27
  35.2 3.5 %collective-permute-start.6 = (bf16[1,32,256]{2,1,0:T(8,128)(2,1)S(1)}, bf16[1,32,256]{2,1,0:T(8,128)(2,1)S(1)}, u32[]{:S(2)}, u32[]{:S(2)}) collective-permute-start(bf16[1,32,256]{2,1,0:T(8,128)(2,1)S(1)} %get-tuple-element.48), channel_id=1, source_target_pairs={{0,2},{2,4},{4,6},{1,3},{3,5},{5,7},{8,10},{10,12},{12,14},{9,11},... | collective-permute-start | bytes 49160 | tf_op jit(solution)/shard_map/ppermute | solution.py:15
  38.7 1.3 collective-permute-start.7
  40.1 4.2 %collective-permute-done.7 = bf16[1,32,256]{2,1,0:T(8,128)(2,1)S(1)} collective-permute-done((bf16[1,32,256]{2,1,0:T(8,128)(2,1)S(1)}, bf16[1,32,256]{2,1,0:T(8,128)(2,1)S(1)}, u32[]{:S(2)}, u32[]{:S(2)}) %collective-permute-start.7) | collective-permute-done | bytes 16416 | tf_op jit(solution)/shard_map/ppermute | solution.py:17
  44.3 1.6 %collective-permute-start.8 = (bf16[18,1,256]{2,1,0:T(2,128)(2,1)S(1)}, bf16[18,1,256]{2,1,0:T(2,128)(2,1)S(1)}, u32[]{:S(2)}, u32[]{:S(2)}) collective-permute-start(bf16[18,1,256]{2,1,0:T(2,128)(2,1)S(1)} %get-tuple-element.35), channel_id=1, source_target_pairs={{0,1},{2,3},{4,5},{6,7},{8,9},{10,11},{12,13},{14,15},{16,17},{18,... | collective-permute-start | bytes 27656 | tf_op jit(solution)/shard_map/ppermute | solution.py:15
  46.0 1.3 collective-permute-start.9
  47.4 4.2 %collective-permute-done.9 = bf16[18,1,256]{2,1,0:T(2,128)(2,1)S(1)} collective-permute-done((bf16[18,1,256]{2,1,0:T(2,128)(2,1)S(1)}, bf16[18,1,256]{2,1,0:T(2,128)(2,1)S(1)}, u32[]{:S(2)}, u32[]{:S(2)}) %collective-permute-start.9) | collective-permute-done | bytes 9248 | tf_op jit(solution)/shard_map/ppermute | solution.py:17
  52.4 1.4 convolution_add_fusion.4
  53.8 1.0 fusion.99
  54.8 1.9 %collective-permute-start.10 = (bf16[16,32,128]{2,1,0:T(8,128)(2,1)S(1)}, bf16[16,32,128]{2,1,0:T(8,128)(2,1)S(1)}, u32[]{:S(2)}, u32[]{:S(2)}) collective-permute-start(bf16[16,32,128]{2,1,0:T(8,128)(2,1)S(1)} %get-tuple-element.12), channel_id=1, source_target_pairs={{0,8},{8,16},{16,24},{1,9},{9,17},{17,25},{2,10},{10,18},{18,26},{... | collective-permute-start | bytes 393224 | tf_op jit(solution)/shard_map/ppermute | solution.py:27
  56.7 4.4 %collective-permute-done.10 = bf16[16,32,128]{2,1,0:T(8,128)(2,1)S(1)} collective-permute-done((bf16[16,32,128]{2,1,0:T(8,128)(2,1)S(1)}, bf16[16,32,128]{2,1,0:T(8,128)(2,1)S(1)}, u32[]{:S(2)}, u32[]{:S(2)}) %collective-permute-start.10) | collective-permute-done | bytes 131104 | tf_op jit(solution)/shard_map/ppermute | solution.py:27
  61.1 3.5 %collective-permute-start.11 = (bf16[1,32,256]{2,1,0:T(8,128)(2,1)S(1)}, bf16[1,32,256]{2,1,0:T(8,128)(2,1)S(1)}, u32[]{:S(2)}, u32[]{:S(2)}) collective-permute-start(bf16[1,32,256]{2,1,0:T(8,128)(2,1)S(1)} %get-tuple-element.46), channel_id=1, source_target_pairs={{0,2},{2,4},{4,6},{1,3},{3,5},{5,7},{8,10},{10,12},{12,14},{9,11},... | collective-permute-start | bytes 49160 | tf_op jit(solution)/shard_map/ppermute | solution.py:15
  64.6 1.3 collective-permute-start.12
  66.0 4.2 %collective-permute-done.12 = bf16[1,32,256]{2,1,0:T(8,128)(2,1)S(1)} collective-permute-done((bf16[1,32,256]{2,1,0:T(8,128)(2,1)S(1)}, bf16[1,32,256]{2,1,0:T(8,128)(2,1)S(1)}, u32[]{:S(2)}, u32[]{:S(2)}) %collective-permute-start.12) | collective-permute-done | bytes 16416 | tf_op jit(solution)/shard_map/ppermute | solution.py:17
  70.3 1.6 %collective-permute-start.13 = (bf16[18,1,256]{2,1,0:T(2,128)(2,1)S(1)}, bf16[18,1,256]{2,1,0:T(2,128)(2,1)S(1)}, u32[]{:S(2)}, u32[]{:S(2)}) collective-permute-start(bf16[18,1,256]{2,1,0:T(2,128)(2,1)S(1)} %get-tuple-element.31), channel_id=1, source_target_pairs={{0,1},{2,3},{4,5},{6,7},{8,9},{10,11},{12,13},{14,15},{16,17},{18,... | collective-permute-start | bytes 27656 | tf_op jit(solution)/shard_map/ppermute | solution.py:15
  71.9 1.3 collective-permute-start.14
  73.3 4.2 %collective-permute-done.14 = bf16[18,1,256]{2,1,0:T(2,128)(2,1)S(1)} collective-permute-done((bf16[18,1,256]{2,1,0:T(2,128)(2,1)S(1)}, bf16[18,1,256]{2,1,0:T(2,128)(2,1)S(1)}, u32[]{:S(2)}, u32[]{:S(2)}) %collective-permute-start.14) | collective-permute-done | bytes 9248 | tf_op jit(solution)/shard_map/ppermute | solution.py:17
  78.3 1.4 convolution_add_fusion.3
  79.7 0.3 fusion.98
  80.1 1.9 %collective-permute-start.15 = (bf16[16,32,128]{2,1,0:T(8,128)(2,1)S(1)}, bf16[16,32,128]{2,1,0:T(8,128)(2,1)S(1)}, u32[]{:S(2)}, u32[]{:S(2)}) collective-permute-start(bf16[16,32,128]{2,1,0:T(8,128)(2,1)S(1)} %get-tuple-element.9), channel_id=1, source_target_pairs={{0,8},{8,16},{16,24},{1,9},{9,17},{17,25},{2,10},{10,18},{18,26},{... | collective-permute-start | bytes 393224 | tf_op jit(solution)/shard_map/ppermute | solution.py:27
  82.0 4.4 %collective-permute-done.15 = bf16[16,32,128]{2,1,0:T(8,128)(2,1)S(1)} collective-permute-done((bf16[16,32,128]{2,1,0:T(8,128)(2,1)S(1)}, bf16[16,32,128]{2,1,0:T(8,128)(2,1)S(1)}, u32[]{:S(2)}, u32[]{:S(2)}) %collective-permute-start.15) | collective-permute-done | bytes 131104 | tf_op jit(solution)/shard_map/ppermute | solution.py:27
  86.3 0.9 bitcast_select_fusion.4
  87.3 1.9 %collective-permute-start.16 = (bf16[1,32,256]{2,1,0:T(8,128)(2,1)S(1)}, bf16[1,32,256]{2,1,0:T(8,128)(2,1)S(1)}, u32[]{:S(2)}, u32[]{:S(2)}) collective-permute-start(bf16[1,32,256]{2,1,0:T(8,128)(2,1)S(1)} %get-tuple-element.44), channel_id=1, source_target_pairs={{0,2},{2,4},{4,6},{1,3},{3,5},{5,7},{8,10},{10,12},{12,14},{9,11},... | collective-permute-start | bytes 49160 | tf_op jit(solution)/shard_map/ppermute | solution.py:15
  89.2 1.3 collective-permute-start.17
  90.6 4.2 %collective-permute-done.17 = bf16[1,32,256]{2,1,0:T(8,128)(2,1)S(1)} collective-permute-done((bf16[1,32,256]{2,1,0:T(8,128)(2,1)S(1)}, bf16[1,32,256]{2,1,0:T(8,128)(2,1)S(1)}, u32[]{:S(2)}, u32[]{:S(2)}) %collective-permute-start.17) | collective-permute-done | bytes 16416 | tf_op jit(solution)/shard_map/ppermute | solution.py:17
  94.9 1.6 %collective-permute-start.18 = (bf16[18,1,256]{2,1,0:T(2,128)(2,1)S(1)}, bf16[18,1,256]{2,1,0:T(2,128)(2,1)S(1)}, u32[]{:S(2)}, u32[]{:S(2)}) collective-permute-start(bf16[18,1,256]{2,1,0:T(2,128)(2,1)S(1)} %get-tuple-element.27), channel_id=1, source_target_pairs={{0,1},{2,3},{4,5},{6,7},{8,9},{10,11},{12,13},{14,15},{16,17},{18,... | collective-permute-start | bytes 27656 | tf_op jit(solution)/shard_map/ppermute | solution.py:15
  96.5 1.3 collective-permute-start.19
  98.0 4.2 %collective-permute-done.19 = bf16[18,1,256]{2,1,0:T(2,128)(2,1)S(1)} collective-permute-done((bf16[18,1,256]{2,1,0:T(2,128)(2,1)S(1)}, bf16[18,1,256]{2,1,0:T(2,128)(2,1)S(1)}, u32[]{:S(2)}, u32[]{:S(2)}) %collective-permute-start.19) | collective-permute-done | bytes 9248 | tf_op jit(solution)/shard_map/ppermute | solution.py:17
  103.0 1.4 convolution_add_fusion.2
  104.3 1.0 fusion.97
  105.3 1.9 %collective-permute-start.20 = (bf16[16,32,128]{2,1,0:T(8,128)(2,1)S(1)}, bf16[16,32,128]{2,1,0:T(8,128)(2,1)S(1)}, u32[]{:S(2)}, u32[]{:S(2)}) collective-permute-start(bf16[16,32,128]{2,1,0:T(8,128)(2,1)S(1)} %get-tuple-element.7), channel_id=1, source_target_pairs={{0,8},{8,16},{16,24},{1,9},{9,17},{17,25},{2,10},{10,18},{18,26},{... | collective-permute-start | bytes 393224 | tf_op jit(solution)/shard_map/ppermute | solution.py:27
  107.3 4.4 %collective-permute-done.20 = bf16[16,32,128]{2,1,0:T(8,128)(2,1)S(1)} collective-permute-done((bf16[16,32,128]{2,1,0:T(8,128)(2,1)S(1)}, bf16[16,32,128]{2,1,0:T(8,128)(2,1)S(1)}, u32[]{:S(2)}, u32[]{:S(2)}) %collective-permute-start.20) | collective-permute-done | bytes 131104 | tf_op jit(solution)/shard_map/ppermute | solution.py:27
  111.6 0.9 bitcast_select_fusion.3
  112.5 1.9 %collective-permute-start.21 = (bf16[1,32,256]{2,1,0:T(8,128)(2,1)S(1)}, bf16[1,32,256]{2,1,0:T(8,128)(2,1)S(1)}, u32[]{:S(2)}, u32[]{:S(2)}) collective-permute-start(bf16[1,32,256]{2,1,0:T(8,128)(2,1)S(1)} %get-tuple-element.42), channel_id=1, source_target_pairs={{0,2},{2,4},{4,6},{1,3},{3,5},{5,7},{8,10},{10,12},{12,14},{9,11},... | collective-permute-start | bytes 49160 | tf_op jit(solution)/shard_map/ppermute | solution.py:15
  114.5 1.3 collective-permute-start.22
  115.9 4.2 %collective-permute-done.22 = bf16[1,32,256]{2,1,0:T(8,128)(2,1)S(1)} collective-permute-done((bf16[1,32,256]{2,1,0:T(8,128)(2,1)S(1)}, bf16[1,32,256]{2,1,0:T(8,128)(2,1)S(1)}, u32[]{:S(2)}, u32[]{:S(2)}) %collective-permute-start.22) | collective-permute-done | bytes 16416 | tf_op jit(solution)/shard_map/ppermute | solution.py:17
  120.1 1.6 %collective-permute-start.23 = (bf16[18,1,256]{2,1,0:T(2,128)(2,1)S(1)}, bf16[18,1,256]{2,1,0:T(2,128)(2,1)S(1)}, u32[]{:S(2)}, u32[]{:S(2)}) collective-permute-start(bf16[18,1,256]{2,1,0:T(2,128)(2,1)S(1)} %get-tuple-element.23), channel_id=1, source_target_pairs={{0,1},{2,3},{4,5},{6,7},{8,9},{10,11},{12,13},{14,15},{16,17},{18,... | collective-permute-start | bytes 27656 | tf_op jit(solution)/shard_map/ppermute | solution.py:15
  121.8 1.3 collective-permute-start.24
  123.2 4.2 %collective-permute-done.24 = bf16[18,1,256]{2,1,0:T(2,128)(2,1)S(1)} collective-permute-done((bf16[18,1,256]{2,1,0:T(2,128)(2,1)S(1)}, bf16[18,1,256]{2,1,0:T(2,128)(2,1)S(1)}, u32[]{:S(2)}, u32[]{:S(2)}) %collective-permute-start.24) | collective-permute-done | bytes 9248 | tf_op jit(solution)/shard_map/ppermute | solution.py:17
  128.2 1.4 convolution_add_fusion.1
  129.6 1.0 fusion.96
  130.7 1.9 %collective-permute-start.25 = (bf16[16,32,128]{2,1,0:T(8,128)(2,1)S(1)}, bf16[16,32,128]{2,1,0:T(8,128)(2,1)S(1)}, u32[]{:S(2)}, u32[]{:S(2)}) collective-permute-start(bf16[16,32,128]{2,1,0:T(8,128)(2,1)S(1)} %get-tuple-element.4), channel_id=1, source_target_pairs={{0,8},{8,16},{16,24},{1,9},{9,17},{17,25},{2,10},{10,18},{18,26},{... | collective-permute-start | bytes 393224 | tf_op jit(solution)/shard_map/ppermute | solution.py:27
  132.6 4.4 %collective-permute-done.25 = bf16[16,32,128]{2,1,0:T(8,128)(2,1)S(1)} collective-permute-done((bf16[16,32,128]{2,1,0:T(8,128)(2,1)S(1)}, bf16[16,32,128]{2,1,0:T(8,128)(2,1)S(1)}, u32[]{:S(2)}, u32[]{:S(2)}) %collective-permute-start.25) | collective-permute-done | bytes 131104 | tf_op jit(solution)/shard_map/ppermute | solution.py:27
  136.9 0.9 bitcast_select_fusion.2
  137.9 1.9 %collective-permute-start.26 = (bf16[1,32,256]{2,1,0:T(8,128)(2,1)S(1)}, bf16[1,32,256]{2,1,0:T(8,128)(2,1)S(1)}, u32[]{:S(2)}, u32[]{:S(2)}) collective-permute-start(bf16[1,32,256]{2,1,0:T(8,128)(2,1)S(1)} %get-tuple-element.40), channel_id=1, source_target_pairs={{0,2},{2,4},{4,6},{1,3},{3,5},{5,7},{8,10},{10,12},{12,14},{9,11},... | collective-permute-start | bytes 49160 | tf_op jit(solution)/shard_map/ppermute | solution.py:15
  139.8 1.3 collective-permute-start.27
  141.2 4.2 %collective-permute-done.27 = bf16[1,32,256]{2,1,0:T(8,128)(2,1)S(1)} collective-permute-done((bf16[1,32,256]{2,1,0:T(8,128)(2,1)S(1)}, bf16[1,32,256]{2,1,0:T(8,128)(2,1)S(1)}, u32[]{:S(2)}, u32[]{:S(2)}) %collective-permute-start.27) | collective-permute-done | bytes 16416 | tf_op jit(solution)/shard_map/ppermute | solution.py:17
  145.5 1.6 %collective-permute-start.28 = (bf16[18,1,256]{2,1,0:T(2,128)(2,1)S(1)}, bf16[18,1,256]{2,1,0:T(2,128)(2,1)S(1)}, u32[]{:S(2)}, u32[]{:S(2)}) collective-permute-start(bf16[18,1,256]{2,1,0:T(2,128)(2,1)S(1)} %get-tuple-element.19), channel_id=1, source_target_pairs={{0,1},{2,3},{4,5},{6,7},{8,9},{10,11},{12,13},{14,15},{16,17},{18,... | collective-permute-start | bytes 27656 | tf_op jit(solution)/shard_map/ppermute | solution.py:15
  147.1 1.3 collective-permute-start.29
  148.6 4.2 %collective-permute-done.29 = bf16[18,1,256]{2,1,0:T(2,128)(2,1)S(1)} collective-permute-done((bf16[18,1,256]{2,1,0:T(2,128)(2,1)S(1)}, bf16[18,1,256]{2,1,0:T(2,128)(2,1)S(1)}, u32[]{:S(2)}, u32[]{:S(2)}) %collective-permute-start.29) | collective-permute-done | bytes 9248 | tf_op jit(solution)/shard_map/ppermute | solution.py:17
  153.6 1.4 convolution_add_fusion
  155.0 0.9 select_bitcast_fusion
  155.9 0.8 select_bitcast_fusion.1
  (109 shorter events, 6.5 us)
Async XLA Ops:
  0.6 26.4 %copy-start = (bf16[1,9,256,512]{3,2,1,0:T(8,128)(2,1)S(1)}, bf16[1,9,256,512]{3,2,1,0:T(8,128)(2,1)}, u32[]{:S(2)}) copy-start(bf16[1,9,256,512]{3,2,1,0:T(8,128)(2,1)} %param.4) | copy-start | bytes 7077892
  0.7 6.4 %collective-permute-start = (bf16[16,32,128]{2,1,0:T(8,128)(2,1)S(1)}, bf16[16,32,128]{2,1,0:T(8,128)(2,1)S(1)}, u32[]{:S(2)}, u32[]{:S(2)}) collective-permute-start(bf16[16,32,128]{2,1,0:T(8,128)(2,1)S(1)} %broadcast_in_dim.12), channel_id=1, source_target_pairs={{0,8},{8,16},{16,24},{1,9},{9,17},{17,25},{2,10},{10,18},{18,26},{... | collective-permute-start | bytes 393224 | tf_op jit(solution)/shard_map/ppermute | solution.py:27
  8.0 4.9 %collective-permute-start.1 = (bf16[1,32,256]{2,1,0:T(8,128)(2,1)S(1)}, bf16[1,32,256]{2,1,0:T(8,128)(2,1)S(1)}, u32[]{:S(2)}, u32[]{:S(2)}) collective-permute-start(bf16[1,32,256]{2,1,0:T(8,128)(2,1)S(1)} %get-tuple-element.50), channel_id=1, source_target_pairs={{0,2},{2,4},{4,6},{1,3},{3,5},{5,7},{8,10},{10,12},{12,14},{9,11},... | collective-permute-start | bytes 49160 | tf_op jit(solution)/shard_map/ppermute | solution.py:15
  11.5 5.6 %collective-permute-start.2 = (bf16[1,32,256]{2,1,0:T(8,128)(2,1)S(1)}, bf16[1,32,256]{2,1,0:T(8,128)(2,1)S(1)}, u32[]{:S(2)}, u32[]{:S(2)}) collective-permute-start(bf16[1,32,256]{2,1,0:T(8,128)(2,1)S(1)} %get-tuple-element.51), channel_id=1, source_target_pairs={{2,0},{4,2},{6,4},{3,1},{5,3},{7,5},{10,8},{12,10},{14,12},{11,9},... | collective-permute-start | bytes 49160 | tf_op jit(solution)/shard_map/ppermute | solution.py:17
  17.2 4.9 %collective-permute-start.3 = (bf16[18,1,256]{2,1,0:T(2,128)(2,1)S(1)}, bf16[18,1,256]{2,1,0:T(2,128)(2,1)S(1)}, u32[]{:S(2)}, u32[]{:S(2)}) collective-permute-start(bf16[18,1,256]{2,1,0:T(2,128)(2,1)S(1)} %get-tuple-element.39), channel_id=1, source_target_pairs={{0,1},{2,3},{4,5},{6,7},{8,9},{10,11},{12,13},{14,15},{16,17},{18,... | collective-permute-start | bytes 27656 | tf_op jit(solution)/shard_map/ppermute | solution.py:15
  20.6 5.7 %collective-permute-start.4 = (bf16[18,1,256]{2,1,0:T(2,128)(2,1)S(1)}, bf16[18,1,256]{2,1,0:T(2,128)(2,1)S(1)}, u32[]{:S(2)}, u32[]{:S(2)}) collective-permute-start(bf16[18,1,256]{2,1,0:T(2,128)(2,1)S(1)} %get-tuple-element.38), channel_id=1, source_target_pairs={{1,0},{3,2},{5,4},{7,6},{9,8},{11,10},{13,12},{15,14},{17,16},{19,... | collective-permute-start | bytes 27656 | tf_op jit(solution)/shard_map/ppermute | solution.py:17
  26.5 0.7 copy-start.6
  27.2 8.0 %copy-start.1 = (bf16[3,16,32,128]{3,2,1,0:T(8,128)(2,1)S(1)}, bf16[3,16,32,128]{3,2,1,0:T(8,128)(2,1)}, u32[]{:S(2)}) copy-start(bf16[3,16,32,128]{3,2,1,0:T(8,128)(2,1)} %param.3) | copy-start | bytes 1179652
  28.8 6.3 %collective-permute-start.5 = (bf16[16,32,128]{2,1,0:T(8,128)(2,1)S(1)}, bf16[16,32,128]{2,1,0:T(8,128)(2,1)S(1)}, u32[]{:S(2)}, u32[]{:S(2)}) collective-permute-start(bf16[16,32,128]{2,1,0:T(8,128)(2,1)S(1)} %get-tuple-element.14), channel_id=1, source_target_pairs={{0,8},{8,16},{16,24},{1,9},{9,17},{17,25},{2,10},{10,18},{18,26},{... | collective-permute-start | bytes 393224 | tf_op jit(solution)/shard_map/ppermute | solution.py:27
  35.2 4.9 %collective-permute-start.6 = (bf16[1,32,256]{2,1,0:T(8,128)(2,1)S(1)}, bf16[1,32,256]{2,1,0:T(8,128)(2,1)S(1)}, u32[]{:S(2)}, u32[]{:S(2)}) collective-permute-start(bf16[1,32,256]{2,1,0:T(8,128)(2,1)S(1)} %get-tuple-element.48), channel_id=1, source_target_pairs={{0,2},{2,4},{4,6},{1,3},{3,5},{5,7},{8,10},{10,12},{12,14},{9,11},... | collective-permute-start | bytes 49160 | tf_op jit(solution)/shard_map/ppermute | solution.py:15
  38.7 5.6 %collective-permute-start.7 = (bf16[1,32,256]{2,1,0:T(8,128)(2,1)S(1)}, bf16[1,32,256]{2,1,0:T(8,128)(2,1)S(1)}, u32[]{:S(2)}, u32[]{:S(2)}) collective-permute-start(bf16[1,32,256]{2,1,0:T(8,128)(2,1)S(1)} %get-tuple-element.49), channel_id=1, source_target_pairs={{2,0},{4,2},{6,4},{3,1},{5,3},{7,5},{10,8},{12,10},{14,12},{11,9},... | collective-permute-start | bytes 49160 | tf_op jit(solution)/shard_map/ppermute | solution.py:17
  44.3 3.1 %collective-permute-start.8 = (bf16[18,1,256]{2,1,0:T(2,128)(2,1)S(1)}, bf16[18,1,256]{2,1,0:T(2,128)(2,1)S(1)}, u32[]{:S(2)}, u32[]{:S(2)}) collective-permute-start(bf16[18,1,256]{2,1,0:T(2,128)(2,1)S(1)} %get-tuple-element.35), channel_id=1, source_target_pairs={{0,1},{2,3},{4,5},{6,7},{8,9},{10,11},{12,13},{14,15},{16,17},{18,... | collective-permute-start | bytes 27656 | tf_op jit(solution)/shard_map/ppermute | solution.py:15
  46.0 5.7 %collective-permute-start.9 = (bf16[18,1,256]{2,1,0:T(2,128)(2,1)S(1)}, bf16[18,1,256]{2,1,0:T(2,128)(2,1)S(1)}, u32[]{:S(2)}, u32[]{:S(2)}) collective-permute-start(bf16[18,1,256]{2,1,0:T(2,128)(2,1)S(1)} %get-tuple-element.34), channel_id=1, source_target_pairs={{1,0},{3,2},{5,4},{7,6},{9,8},{11,10},{13,12},{15,14},{17,16},{19,... | collective-permute-start | bytes 27656 | tf_op jit(solution)/shard_map/ppermute | solution.py:17
  54.8 6.3 %collective-permute-start.10 = (bf16[16,32,128]{2,1,0:T(8,128)(2,1)S(1)}, bf16[16,32,128]{2,1,0:T(8,128)(2,1)S(1)}, u32[]{:S(2)}, u32[]{:S(2)}) collective-permute-start(bf16[16,32,128]{2,1,0:T(8,128)(2,1)S(1)} %get-tuple-element.12), channel_id=1, source_target_pairs={{0,8},{8,16},{16,24},{1,9},{9,17},{17,25},{2,10},{10,18},{18,26},{... | collective-permute-start | bytes 393224 | tf_op jit(solution)/shard_map/ppermute | solution.py:27
  61.1 4.9 %collective-permute-start.11 = (bf16[1,32,256]{2,1,0:T(8,128)(2,1)S(1)}, bf16[1,32,256]{2,1,0:T(8,128)(2,1)S(1)}, u32[]{:S(2)}, u32[]{:S(2)}) collective-permute-start(bf16[1,32,256]{2,1,0:T(8,128)(2,1)S(1)} %get-tuple-element.46), channel_id=1, source_target_pairs={{0,2},{2,4},{4,6},{1,3},{3,5},{5,7},{8,10},{10,12},{12,14},{9,11},... | collective-permute-start | bytes 49160 | tf_op jit(solution)/shard_map/ppermute | solution.py:15
  64.6 5.6 %collective-permute-start.12 = (bf16[1,32,256]{2,1,0:T(8,128)(2,1)S(1)}, bf16[1,32,256]{2,1,0:T(8,128)(2,1)S(1)}, u32[]{:S(2)}, u32[]{:S(2)}) collective-permute-start(bf16[1,32,256]{2,1,0:T(8,128)(2,1)S(1)} %get-tuple-element.47), channel_id=1, source_target_pairs={{2,0},{4,2},{6,4},{3,1},{5,3},{7,5},{10,8},{12,10},{14,12},{11,9},... | collective-permute-start | bytes 49160 | tf_op jit(solution)/shard_map/ppermute | solution.py:17
  70.3 3.1 %collective-permute-start.13 = (bf16[18,1,256]{2,1,0:T(2,128)(2,1)S(1)}, bf16[18,1,256]{2,1,0:T(2,128)(2,1)S(1)}, u32[]{:S(2)}, u32[]{:S(2)}) collective-permute-start(bf16[18,1,256]{2,1,0:T(2,128)(2,1)S(1)} %get-tuple-element.31), channel_id=1, source_target_pairs={{0,1},{2,3},{4,5},{6,7},{8,9},{10,11},{12,13},{14,15},{16,17},{18,... | collective-permute-start | bytes 27656 | tf_op jit(solution)/shard_map/ppermute | solution.py:15
  71.9 5.7 %collective-permute-start.14 = (bf16[18,1,256]{2,1,0:T(2,128)(2,1)S(1)}, bf16[18,1,256]{2,1,0:T(2,128)(2,1)S(1)}, u32[]{:S(2)}, u32[]{:S(2)}) collective-permute-start(bf16[18,1,256]{2,1,0:T(2,128)(2,1)S(1)} %get-tuple-element.30), channel_id=1, source_target_pairs={{1,0},{3,2},{5,4},{7,6},{9,8},{11,10},{13,12},{15,14},{17,16},{19,... | collective-permute-start | bytes 27656 | tf_op jit(solution)/shard_map/ppermute | solution.py:17
  78.3 1.4 copy-start.2
  80.1 6.3 %collective-permute-start.15 = (bf16[16,32,128]{2,1,0:T(8,128)(2,1)S(1)}, bf16[16,32,128]{2,1,0:T(8,128)(2,1)S(1)}, u32[]{:S(2)}, u32[]{:S(2)}) collective-permute-start(bf16[16,32,128]{2,1,0:T(8,128)(2,1)S(1)} %get-tuple-element.9), channel_id=1, source_target_pairs={{0,8},{8,16},{16,24},{1,9},{9,17},{17,25},{2,10},{10,18},{18,26},{... | collective-permute-start | bytes 393224 | tf_op jit(solution)/shard_map/ppermute | solution.py:27
  87.3 3.4 %collective-permute-start.16 = (bf16[1,32,256]{2,1,0:T(8,128)(2,1)S(1)}, bf16[1,32,256]{2,1,0:T(8,128)(2,1)S(1)}, u32[]{:S(2)}, u32[]{:S(2)}) collective-permute-start(bf16[1,32,256]{2,1,0:T(8,128)(2,1)S(1)} %get-tuple-element.44), channel_id=1, source_target_pairs={{0,2},{2,4},{4,6},{1,3},{3,5},{5,7},{8,10},{10,12},{12,14},{9,11},... | collective-permute-start | bytes 49160 | tf_op jit(solution)/shard_map/ppermute | solution.py:15
  89.2 5.6 %collective-permute-start.17 = (bf16[1,32,256]{2,1,0:T(8,128)(2,1)S(1)}, bf16[1,32,256]{2,1,0:T(8,128)(2,1)S(1)}, u32[]{:S(2)}, u32[]{:S(2)}) collective-permute-start(bf16[1,32,256]{2,1,0:T(8,128)(2,1)S(1)} %get-tuple-element.45), channel_id=1, source_target_pairs={{2,0},{4,2},{6,4},{3,1},{5,3},{7,5},{10,8},{12,10},{14,12},{11,9},... | collective-permute-start | bytes 49160 | tf_op jit(solution)/shard_map/ppermute | solution.py:17
  94.9 3.1 %collective-permute-start.18 = (bf16[18,1,256]{2,1,0:T(2,128)(2,1)S(1)}, bf16[18,1,256]{2,1,0:T(2,128)(2,1)S(1)}, u32[]{:S(2)}, u32[]{:S(2)}) collective-permute-start(bf16[18,1,256]{2,1,0:T(2,128)(2,1)S(1)} %get-tuple-element.27), channel_id=1, source_target_pairs={{0,1},{2,3},{4,5},{6,7},{8,9},{10,11},{12,13},{14,15},{16,17},{18,... | collective-permute-start | bytes 27656 | tf_op jit(solution)/shard_map/ppermute | solution.py:15
  96.5 5.7 %collective-permute-start.19 = (bf16[18,1,256]{2,1,0:T(2,128)(2,1)S(1)}, bf16[18,1,256]{2,1,0:T(2,128)(2,1)S(1)}, u32[]{:S(2)}, u32[]{:S(2)}) collective-permute-start(bf16[18,1,256]{2,1,0:T(2,128)(2,1)S(1)} %get-tuple-element.26), channel_id=1, source_target_pairs={{1,0},{3,2},{5,4},{7,6},{9,8},{11,10},{13,12},{15,14},{17,16},{19,... | collective-permute-start | bytes 27656 | tf_op jit(solution)/shard_map/ppermute | solution.py:17
  105.3 6.3 %collective-permute-start.20 = (bf16[16,32,128]{2,1,0:T(8,128)(2,1)S(1)}, bf16[16,32,128]{2,1,0:T(8,128)(2,1)S(1)}, u32[]{:S(2)}, u32[]{:S(2)}) collective-permute-start(bf16[16,32,128]{2,1,0:T(8,128)(2,1)S(1)} %get-tuple-element.7), channel_id=1, source_target_pairs={{0,8},{8,16},{16,24},{1,9},{9,17},{17,25},{2,10},{10,18},{18,26},{... | collective-permute-start | bytes 393224 | tf_op jit(solution)/shard_map/ppermute | solution.py:27
  112.5 3.4 %collective-permute-start.21 = (bf16[1,32,256]{2,1,0:T(8,128)(2,1)S(1)}, bf16[1,32,256]{2,1,0:T(8,128)(2,1)S(1)}, u32[]{:S(2)}, u32[]{:S(2)}) collective-permute-start(bf16[1,32,256]{2,1,0:T(8,128)(2,1)S(1)} %get-tuple-element.42), channel_id=1, source_target_pairs={{0,2},{2,4},{4,6},{1,3},{3,5},{5,7},{8,10},{10,12},{12,14},{9,11},... | collective-permute-start | bytes 49160 | tf_op jit(solution)/shard_map/ppermute | solution.py:15
  114.5 5.6 %collective-permute-start.22 = (bf16[1,32,256]{2,1,0:T(8,128)(2,1)S(1)}, bf16[1,32,256]{2,1,0:T(8,128)(2,1)S(1)}, u32[]{:S(2)}, u32[]{:S(2)}) collective-permute-start(bf16[1,32,256]{2,1,0:T(8,128)(2,1)S(1)} %get-tuple-element.43), channel_id=1, source_target_pairs={{2,0},{4,2},{6,4},{3,1},{5,3},{7,5},{10,8},{12,10},{14,12},{11,9},... | collective-permute-start | bytes 49160 | tf_op jit(solution)/shard_map/ppermute | solution.py:17
  120.1 3.1 %collective-permute-start.23 = (bf16[18,1,256]{2,1,0:T(2,128)(2,1)S(1)}, bf16[18,1,256]{2,1,0:T(2,128)(2,1)S(1)}, u32[]{:S(2)}, u32[]{:S(2)}) collective-permute-start(bf16[18,1,256]{2,1,0:T(2,128)(2,1)S(1)} %get-tuple-element.23), channel_id=1, source_target_pairs={{0,1},{2,3},{4,5},{6,7},{8,9},{10,11},{12,13},{14,15},{16,17},{18,... | collective-permute-start | bytes 27656 | tf_op jit(solution)/shard_map/ppermute | solution.py:15
  121.8 5.7 %collective-permute-start.24 = (bf16[18,1,256]{2,1,0:T(2,128)(2,1)S(1)}, bf16[18,1,256]{2,1,0:T(2,128)(2,1)S(1)}, u32[]{:S(2)}, u32[]{:S(2)}) collective-permute-start(bf16[18,1,256]{2,1,0:T(2,128)(2,1)S(1)} %get-tuple-element.22), channel_id=1, source_target_pairs={{1,0},{3,2},{5,4},{7,6},{9,8},{11,10},{13,12},{15,14},{17,16},{19,... | collective-permute-start | bytes 27656 | tf_op jit(solution)/shard_map/ppermute | solution.py:17
  128.2 1.4 copy-start.5
  130.7 6.3 %collective-permute-start.25 = (bf16[16,32,128]{2,1,0:T(8,128)(2,1)S(1)}, bf16[16,32,128]{2,1,0:T(8,128)(2,1)S(1)}, u32[]{:S(2)}, u32[]{:S(2)}) collective-permute-start(bf16[16,32,128]{2,1,0:T(8,128)(2,1)S(1)} %get-tuple-element.4), channel_id=1, source_target_pairs={{0,8},{8,16},{16,24},{1,9},{9,17},{17,25},{2,10},{10,18},{18,26},{... | collective-permute-start | bytes 393224 | tf_op jit(solution)/shard_map/ppermute | solution.py:27
  137.9 3.4 %collective-permute-start.26 = (bf16[1,32,256]{2,1,0:T(8,128)(2,1)S(1)}, bf16[1,32,256]{2,1,0:T(8,128)(2,1)S(1)}, u32[]{:S(2)}, u32[]{:S(2)}) collective-permute-start(bf16[1,32,256]{2,1,0:T(8,128)(2,1)S(1)} %get-tuple-element.40), channel_id=1, source_target_pairs={{0,2},{2,4},{4,6},{1,3},{3,5},{5,7},{8,10},{10,12},{12,14},{9,11},... | collective-permute-start | bytes 49160 | tf_op jit(solution)/shard_map/ppermute | solution.py:15
  139.8 5.6 %collective-permute-start.27 = (bf16[1,32,256]{2,1,0:T(8,128)(2,1)S(1)}, bf16[1,32,256]{2,1,0:T(8,128)(2,1)S(1)}, u32[]{:S(2)}, u32[]{:S(2)}) collective-permute-start(bf16[1,32,256]{2,1,0:T(8,128)(2,1)S(1)} %get-tuple-element.41), channel_id=1, source_target_pairs={{2,0},{4,2},{6,4},{3,1},{5,3},{7,5},{10,8},{12,10},{14,12},{11,9},... | collective-permute-start | bytes 49160 | tf_op jit(solution)/shard_map/ppermute | solution.py:17
  145.5 3.1 %collective-permute-start.28 = (bf16[18,1,256]{2,1,0:T(2,128)(2,1)S(1)}, bf16[18,1,256]{2,1,0:T(2,128)(2,1)S(1)}, u32[]{:S(2)}, u32[]{:S(2)}) collective-permute-start(bf16[18,1,256]{2,1,0:T(2,128)(2,1)S(1)} %get-tuple-element.19), channel_id=1, source_target_pairs={{0,1},{2,3},{4,5},{6,7},{8,9},{10,11},{12,13},{14,15},{16,17},{18,... | collective-permute-start | bytes 27656 | tf_op jit(solution)/shard_map/ppermute | solution.py:15
  147.1 5.7 %collective-permute-start.29 = (bf16[18,1,256]{2,1,0:T(2,128)(2,1)S(1)}, bf16[18,1,256]{2,1,0:T(2,128)(2,1)S(1)}, u32[]{:S(2)}, u32[]{:S(2)}) collective-permute-start(bf16[18,1,256]{2,1,0:T(2,128)(2,1)S(1)} %get-tuple-element.18), channel_id=1, source_target_pairs={{1,0},{3,2},{5,4},{7,6},{9,8},{11,10},{13,12},{15,14},{17,16},{19,... | collective-permute-start | bytes 27656 | tf_op jit(solution)/shard_map/ppermute | solution.py:17
  153.5 1.4 copy-start.3
  153.6 1.4 copy-start.4
where the time goes:
time: 158 us; the launch traced here: 157 us
  waiting for transfers between devices  78.2 us (49%)
  starting transfers between devices  54.9 us (35%)
  other arithmetic  11.1 us (7%)
  matrix products  8.27 us (5%)
  local copies, waits for them, and re-layouts  2.58 us (2%)
  between operations  1.59 us (1%)
    ppermute x12, waiting for transfers between devices, with_halo(): lax.ppermute(head, axis, [((i + 1) % count, i) for i in range(ends)])  50.5 us
    ppermute x12, starting transfers between devices, with_halo(): lax.ppermute(tail, axis, [(i, (i + 1) % count) for i in range(ends)])  27.8 us
    ppermute x6, waiting for transfers between devices, passed_along(): lax.ppermute(value, axis, [(source, source + steps) for source in range(i...  26.1 us
    ppermute x12, starting transfers between devices, with_halo(): lax.ppermute(head, axis, [((i + 1) % count, i) for i in range(ends)])  15.5 us
    ppermute x6, starting transfers between devices, passed_along(): lax.ppermute(value, axis, [(source, source + steps) for source in range(i...  11.6 us
    dot_general x6, matrix products, shards(): jnp.dot(patches(padded, rows, cols), stacked_kernel, preferred_element_ty...  8.27 us
    select_n x6, other arithmetic, shards(): jnp.where(section_pos == 0, frames[min(clock, steps_in - 1)], incoming)  3.73 us
    select_n x5, other arithmetic, shards(): hidden = jnp.where(active, new_hidden, hidden)  3.61 us
  transfers between devices with their start and end apart: 30, of which 30 were waited for; matrix products, arithmetic and copies ran while one was open for 0% of the time, Pallas kernels for 0%

commit v1 on v0

v1 whole, which is shorter than its diff:
```python
import jax
import jax.numpy as jnp
from jax import lax
from jax.experimental import pallas as pl
from jax.experimental.pallas import tpu as pltpu
from jax.sharding import PartitionSpec as P

MESH = pl.DeviceIdType.MESH
DIRS = [(dr, dc) for dr in (-1, 0, 1) for dc in (-1, 0, 1) if (dr, dc) != (0, 0)]
CHUNK = 4


def sigmoid(v):
    return 0.5 * jnp.tanh(0.5 * v) + 0.5


def slot(dr, dc):
    return (dr + 1) * 3 + (dc + 1)


def body(sizes, frames, weight, bias, hid_out, cell_out,
         xc, xe, hc, he, col_x, col_h, w, ax, ah, acc,
         local_sem, send_sem, xrecv, hrecv):
    nsec, nrow, ncol = sizes
    steps, rows, cols, width = frames.shape
    sec, row, col = lax.axis_index("section"), lax.axis_index("row"), lax.axis_index("col")

    def load_frame(t):
        return pltpu.make_async_copy(frames.at[t], xc.at[t, pl.ds(1, rows)], local_sem.at[t])

    load_w = pltpu.make_async_copy(weight.at[0], w, local_sem.at[steps])

    @pl.when(sec == 0)
    def _():
        for t in range(steps):
            load_frame(t).start()

    load_w.start()

    def there(dr, dc):
        ok = sec >= 0
        if dr:
            ok = (row > 0) if dr < 0 else (row < nrow - 1)
        if dc:
            okc = (col > 0) if dc < 0 else (col < ncol - 1)
            ok = jnp.logical_and(ok, okc) if dr else okc
        return ok

    def device(ds, dr, dc):
        return {"section": sec + ds, "row": row + dr, "col": col + dc}

    zrow = jnp.zeros((cols, width), jnp.bfloat16)
    for buf, edge in ((xc, xe), (hc, he)):
        for t in range(edge.shape[0]):
            buf[t, 0] = zrow
            buf[t, rows + 1] = zrow
            edge[t] = jnp.zeros(edge.shape[1:], jnp.bfloat16)

    barrier = pltpu.get_barrier_semaphore()
    for ds in (-1, 0, 1):
        okd = (sec > 0) if ds < 0 else (sec < nsec - 1)
        if ds:
            @pl.when(okd)
            def _(ds=ds):
                pl.semaphore_signal(barrier, inc=1, device_id=device(ds, 0, 0), device_id_type=MESH)
        for dr, dc in DIRS:
            ok = there(dr, dc)
            if ds:
                ok = jnp.logical_and(ok, okd)

            @pl.when(ok)
            def _(ds=ds, dr=dr, dc=dc):
                pl.semaphore_signal(barrier, inc=1, device_id=device(ds, dr, dc), device_id_type=MESH)

    def extent(pos, count):
        return 1 + jnp.where(pos > 0, 1, 0) + jnp.where(pos < count - 1, 1, 0)

    pl.semaphore_wait(barrier, extent(sec, nsec) * extent(row, nrow) * extent(col, ncol) - 1)

    def halo_copy(center, colbuf, t, kind, ds, dr, dc, to_c, to_e, recv):
        if dc == 0:
            src = center.at[t, rows if dr > 0 else 1]
            dst = to_c.at[t, 0 if dr > 0 else rows + 1]
        else:
            src = colbuf.at[t, 1 if dc > 0 else 0]
            dst = to_e.at[t, (0 if dc > 0 else 3) + (1 - dr)]
        return pltpu.make_async_remote_copy(
            src_ref=src, dst_ref=dst,
            send_sem=send_sem.at[t, kind, slot(dr, dc)],
            recv_sem=recv.at[t, slot(-dr, -dc)],
            device_id=device(ds, dr, dc), device_id_type=MESH,
        )

    def halo_sends(act, center, colbuf, t, kind, ds, to_c, to_e, recv):
        for dr, dc in DIRS:
            @pl.when(there(dr, dc))
            def _(dr=dr, dc=dc):
                copy = halo_copy(center, colbuf, t, kind, ds, dr, dc, to_c, to_e, recv)
                copy.start() if act == "start" else copy.wait_send()

    def halo_waits(t, to_c, to_e, recv):
        for dr, dc in DIRS:
            @pl.when(there(dr, dc))
            def _(dr=dr, dc=dc):
                if dc == 0:
                    dst = to_c.at[t, 0 if dr < 0 else rows + 1]
                else:
                    dst = to_e.at[t, (0 if dc < 0 else 3) + (1 + dr)]
                pltpu.make_async_remote_copy(
                    src_ref=dst, dst_ref=dst,
                    send_sem=send_sem.at[t, 0, slot(0, 0)],
                    recv_sem=recv.at[t, slot(dr, dc)],
                    device_id=device(0, dr, dc), device_id_type=MESH,
                ).wait_recv()

    def center_copy(t):
        return pltpu.make_async_remote_copy(
            src_ref=hc.at[t, pl.ds(1, rows)], dst_ref=xc.at[t, pl.ds(1, rows)],
            send_sem=send_sem.at[t, 1, slot(0, 0)], recv_sem=xrecv.at[t, slot(0, 0)],
            device_id=device(1, 0, 0), device_id_type=MESH,
        )

    def stage_columns(center, t, colbuf):
        value = center[t, pl.ds(1, rows)].astype(jnp.float32)
        colbuf[t, 0] = value[:, 0, :].astype(jnp.bfloat16)
        colbuf[t, 1] = value[:, cols - 1, :].astype(jnp.bfloat16)

    @pl.when(sec == 0)
    def _():
        for t in range(steps):
            load_frame(t).wait()
            stage_columns(xc, t, col_x)
            halo_sends("start", xc, col_x, t, 2, 0, xc, xe, xrecv)

    place = lax.broadcasted_iota(jnp.int32, (cols, width), 0)

    def assemble(center, edge, t, out):
        ends = [edge[t, k].astype(jnp.float32) for k in range(6)]
        for r in range(rows + 2):
            line = center[t, r]
            wide = line.astype(jnp.float32)
            halos = []
            for side in (0, 3):
                if r == 0:
                    halos.append(ends[side][rows - 1:rows])
                elif r == rows + 1:
                    halos.append(ends[side + 2][0:1])
                else:
                    halos.append(ends[side + 1][r - 1:r])
            before = jnp.where(place == 0, halos[0], pltpu.roll(wide, 1, 0))
            after = jnp.where(place == cols - 1, halos[1], pltpu.roll(wide, cols - 1, 0))
            out[r, :, 0:width] = before.astype(jnp.bfloat16)
            out[r, :, width:2 * width] = line
            out[r, :, 2 * width:3 * width] = after.astype(jnp.bfloat16)

    def patches(a, first, count):
        return jnp.concatenate(
            [a[first + k:first + k + count].reshape(count * cols, 3 * width) for k in range(3)], axis=-1
        )

    def kernel_of(half):
        return w[:, half * width:(half + 1) * width, :].reshape(9 * width, 4 * width)

    for t in range(steps):
        if t > 0:
            halo_waits(t - 1, hc, he, hrecv)
            assemble(hc, he, t - 1, ah)
            acc[...] = jnp.dot(patches(ah, 0, rows), kernel_of(1), preferred_element_type=jnp.float32)

        @pl.when(sec > 0)
        def _(t=t):
            center = xc.at[t, pl.ds(1, rows)]
            pltpu.make_async_remote_copy(
                src_ref=center, dst_ref=center, send_sem=send_sem.at[t, 0, slot(0, 0)],
                recv_sem=xrecv.at[t, slot(0, 0)], device_id=device(-1, 0, 0), device_id_type=MESH,
            ).wait_recv()

        halo_waits(t, xc, xe, xrecv)
        assemble(xc, xe, t, ax)
        if t == 0:
            load_w.wait()
        for r in range(0, rows, CHUNK):
            part = pl.ds(r * cols, CHUNK * cols)
            pre = jnp.dot(patches(ax, r, CHUNK), kernel_of(0), preferred_element_type=jnp.float32)
            pre = pre + bias[...]
            if t > 0:
                pre = pre + acc[part]
            gate_in = sigmoid(pre[:, :width])
            cand = jnp.tanh(pre[:, 2 * width:3 * width])
            cell = gate_in * cand
            area = pl.ds(r, CHUNK)
            if t > 0:
                old = cell_out[0, area].reshape(CHUNK * cols, width)
                cell = sigmoid(pre[:, width:2 * width]) * old + cell
            hidden = sigmoid(pre[:, 3 * width:]) * jnp.tanh(cell)
            cell_out[0, area] = cell.reshape(CHUNK, cols, width)
            hidden = hidden.astype(jnp.bfloat16).reshape(CHUNK, cols, width)
            hc[t, pl.ds(r + 1, CHUNK)] = hidden
            if t == steps - 1:
                hid_out[0, area] = hidden
        stage_columns(hc, t, col_h)

        @pl.when(sec < nsec - 1)
        def _(t=t):
            center_copy(t).start()
            halo_sends("start", hc, col_h, t, 1, 1, xc, xe, xrecv)

        if t < steps - 1:
            halo_sends("start", hc, col_h, t, 0, 0, hc, he, hrecv)

    @pl.when(sec == 0)
    def _():
        for t in range(steps):
            halo_sends("wait", xc, col_x, t, 2, 0, xc, xe, xrecv)

    @pl.when(sec < nsec - 1)
    def _():
        for t in range(steps):
            center_copy(t).wait_send()
            halo_sends("wait", hc, col_h, t, 1, 1, xc, xe, xrecv)

    for t in range(steps - 1):
        halo_sends("wait", hc, col_h, t, 0, 0, hc, he, hrecv)


def solution(mesh):
    sizes = (mesh.shape["section"], mesh.shape["row"], mesh.shape["col"])

    def step(frames, weight, bias):
        steps, rows, cols, width = frames.shape
        vmem = pl.BlockSpec(memory_space=pltpu.VMEM)
        hbm = pl.BlockSpec(memory_space=pl.ANY)
        bf16 = jnp.bfloat16
        return pl.pallas_call(
            lambda *refs: body(sizes, *refs),
            out_shape=(
                jax.ShapeDtypeStruct((1, rows, cols, width), bf16),
                jax.ShapeDtypeStruct((1, rows, cols, width), jnp.float32),
            ),
            in_specs=[hbm, hbm, vmem],
            out_specs=(vmem, vmem),
            scratch_shapes=[
                pltpu.VMEM((steps, rows + 2, cols, width), bf16),
                pltpu.VMEM((steps, 6, rows, width), bf16),
                pltpu.VMEM((steps, rows + 2, cols, width), bf16),
                pltpu.VMEM((steps, 6, rows, width), bf16),
                pltpu.VMEM((steps, 2, rows, width), bf16),
                pltpu.VMEM((steps, 2, rows, width), bf16),
                pltpu.VMEM(weight.shape[1:], bf16),
                pltpu.VMEM((rows + 2, cols, 3 * width), bf16),
                pltpu.VMEM((rows + 2, cols, 3 * width), bf16),
                pltpu.VMEM((rows * cols, 4 * width), jnp.float32),
                pltpu.SemaphoreType.DMA((steps + 1,)),
                pltpu.SemaphoreType.DMA((steps, 3, 9)),
                pltpu.SemaphoreType.DMA((steps, 9)),
                pltpu.SemaphoreType.DMA((steps, 9)),
            ],
            compiler_params=pltpu.CompilerParams(collective_id=0, has_side_effects=True),
        )(frames, weight, bias)

    return jax.shard_map(
        step,
        mesh=mesh,
        in_specs=(P(None, "row", "col", None), P("section", None, None, None), P("section", None)),
        out_specs=(P("section", "row", "col", None), P("section", "row", "col", None)),
        check_vma=False,
    )
```

time: 158 us -> 36.8 us (0.23)
  the two profiles are of different devices: /device:TPU:2 before, /device:TPU:3 now
where the time goes in v1:
time: 36.8 us; the launch traced here: 36.6 us
  Pallas kernels  32.8 us (89%)
  local copies, waits for them, and re-layouts  3.24 us (9%)
  between operations  0.64 us (2%)
    pallas_call x1, Pallas kernels, step(): pl.pallas_call(lambda *refs: body(sizes, *refs), out_shape=(jax.ShapeDtyp...  32.8 us
    unnamed x2, local copies, waits for them, and re-layouts  3.24 us

profile of v1, /device:TPU:3, one launch (start us, length us, event | category | flops | bytes accessed | tf_op | source)
XLA Modules:
  0.0 36.6 jit_solution(6486397108645086078)
XLA Ops:
  0.6 32.8 %shard_map.50 = (bf16[1,16,32,128]{3,2,1,0:T(8,128)(2,1)}, f32[1,16,32,128]{3,2,1,0:T(8,128)}) custom-call(bf16[3,16,32,128]{3,2,1,0:T(8,128)(2,1)} %refs_0_.1, bf16[1,9,256,512]{3,2,1,0:T(8,128)(2,1)} %refs_1_.1, f32[1,512]{1,0:T(1,128)} %refs_2_.1), custom_call_target="tpu_custom_call" | custom-call | tf_op jit(solution)/shard_map/pallas_call | solution.py:234
  33.4 1.6 %copy.7 = bf16[1,16,32,128]{3,2,1,0:T(8,128)(2,1)} copy(bf16[1,16,32,128]{3,2,1,0:T(8,128)(2,1)} %get-tuple-element.4) | data formatting | bytes 262144
  35.0 1.7 %copy.8 = f32[1,16,32,128]{3,2,1,0:T(8,128)} copy(f32[1,16,32,128]{3,2,1,0:T(8,128)} %get-tuple-element.5) | data formatting | bytes 524288

commit v2 on v0

v2 whole, which is shorter than its diff:
```python
import jax
import jax.numpy as jnp
from jax import lax
from jax.experimental import pallas as pl
from jax.experimental.pallas import tpu as pltpu
from jax.sharding import PartitionSpec as P

MESH = pl.DeviceIdType.MESH
DIRS = [(dr, dc) for dr in (-1, 0, 1) for dc in (-1, 0, 1) if (dr, dc) != (0, 0)]
PAD = 8
CHUNK = 8


def sigmoid(v):
    return 0.5 * jnp.tanh(0.5 * v) + 0.5


def slot(dr, dc):
    return (dr + 1) * 3 + (dc + 1)


def body(sizes, frames, weight, bias, hid_out, cell_out,
         xc, xe, fe, hc, he, col_x, col_h, w, ax, ah, acc, cell_mem,
         local_sem, send_sem, frecv, xrecv, hrecv):
    nsec, nrow, ncol = sizes
    steps, rows, cols, width = frames.shape
    high = rows + 2 * PAD
    sec, row, col = lax.axis_index("section"), lax.axis_index("row"), lax.axis_index("col")

    def load_frame(t):
        return pltpu.make_async_copy(frames.at[t], xc.at[t, pl.ds(PAD, rows)], local_sem.at[t])

    load_w = pltpu.make_async_copy(weight.at[0], w, local_sem.at[steps])

    @pl.when(sec == 0)
    def _():
        for t in range(steps):
            load_frame(t).start()

    load_w.start()

    def there(dr, dc):
        ok = sec >= 0
        if dr:
            ok = (row > 0) if dr < 0 else (row < nrow - 1)
        if dc:
            okc = (col > 0) if dc < 0 else (col < ncol - 1)
            ok = jnp.logical_and(ok, okc) if dr else okc
        return ok

    def device(ds, dr, dc):
        return {"section": sec + ds, "row": row + dr, "col": col + dc}

    @pl.when(sec == 0)
    def _():
        for t in range(steps):
            fe[t] = jnp.zeros(fe.shape[1:], jnp.bfloat16)
            xc[t, 0:PAD] = jnp.zeros((PAD, cols, width), jnp.bfloat16)
            xc[t, PAD + rows:high] = jnp.zeros((PAD, cols, width), jnp.bfloat16)

    for t in range(steps):
        xe[t] = jnp.zeros(xe.shape[1:], jnp.bfloat16)
        he[t] = jnp.zeros(he.shape[1:], jnp.bfloat16)

    barrier = pltpu.get_barrier_semaphore()
    for ds in (-1, 0, 1):
        okd = (sec > 0) if ds < 0 else (sec < nsec - 1) if ds > 0 else (sec == 0)
        for dr, dc in [(0, 0)] + DIRS:
            if (ds == 0 and (dr, dc) == (0, 0)) or (ds and dr):
                continue
            ok = there(dr, dc)
            if ds or dr:
                ok = jnp.logical_and(ok, okd)

            @pl.when(ok)
            def _(ds=ds, dr=dr, dc=dc):
                pl.semaphore_signal(barrier, inc=1, device_id=device(ds, dr, dc), device_id_type=MESH)

    def extent(pos, count):
        return 1 + jnp.where(pos > 0, 1, 0) + jnp.where(pos < count - 1, 1, 0)

    wide_cols = extent(col, ncol)
    extra = jnp.where(sec == 0, (extent(row, nrow) - 1) * wide_cols, 0)
    pl.semaphore_wait(barrier, extent(sec, nsec) * wide_cols - 1 + extra)

    top = jnp.where(row > 0, 1.0, 0.0)
    bottom = jnp.where(row < nrow - 1, 1.0, 0.0)
    place = lax.broadcasted_iota(jnp.int32, (cols, width), 0)

    def remote(src, dst, send, recv, ds, dr, dc):
        return pltpu.make_async_remote_copy(
            src_ref=src, dst_ref=dst, send_sem=send, recv_sem=recv,
            device_id=device(ds, dr, dc), device_id_type=MESH,
        )

    def stage_columns(value, store):
        value = value.astype(jnp.float32)
        store[0] = value[:, 0, :].astype(jnp.bfloat16)
        store[1] = value[:, cols - 1, :].astype(jnp.bfloat16)

    def assemble(center, ends, t, first, last, out):
        for r in range(first, last):
            line = center[t, r]
            wide = line.astype(jnp.float32)
            before = jnp.where(place == 0, ends[0][r:r + 1], pltpu.roll(wide, 1, 0))
            after = jnp.where(place == cols - 1, ends[1][r:r + 1], pltpu.roll(wide, cols - 1, 0))
            out[r, :, 0:width] = before.astype(jnp.bfloat16)
            out[r, :, width:2 * width] = line
            out[r, :, 2 * width:3 * width] = after.astype(jnp.bfloat16)

    def patches(a, first, count):
        return jnp.concatenate(
            [a[first + k:first + k + count].reshape(count * cols, 3 * width) for k in (-1, 0, 1)], axis=-1
        )

    def kernel_of(half):
        return w[:, half * width:(half + 1) * width, :].reshape(9 * width, 4 * width)

    def column_copy(t, kind, ds, dc, to, recv):
        side = 1 if dc > 0 else 0
        return remote(col_h.at[t, side], to.at[t, 1 - side], send_sem.at[t, kind, side],
                      recv.at[t, 1 - side], ds, 0, dc)

    def pieces(first, last):
        return [(r, min(CHUNK, last - r)) for r in range(first, last, CHUNK)]

    def block_copy(t, n, r, count, ds):
        part = pl.ds(r, count)
        return remote(hc.at[t, part], xc.at[t, part], send_sem.at[t, 1, 2 + n], xrecv.at[t, 2 + n], ds, 0, 0)

    def frame_copy(t, reach, dr, dc):
        if dc == 0:
            src = frames.at[t, pl.ds(0 if dr < 0 else rows - reach, reach)]
            dst = xc.at[t, pl.ds(PAD + rows if dr < 0 else PAD - reach, reach)]
        else:
            src = col_x.at[t, 1 if dc > 0 else 0]
            dst = fe.at[t, (0 if dc > 0 else 3) + (1 - dr)]
        return remote(src, dst, send_sem.at[t, 2, slot(dr, dc)], frecv.at[t, slot(-dr, -dc)], 0, dr, dc)

    def frame_wait(t, reach, dr, dc):
        if dc == 0:
            dst = xc.at[t, pl.ds(PAD - reach if dr < 0 else PAD + rows, reach)]
        else:
            dst = fe.at[t, (0 if dc < 0 else 3) + (1 + dr)]
        remote(dst, dst, send_sem.at[t, 0, 0], frecv.at[t, slot(dr, dc)], 0, dr, dc).wait_recv()

    def section(s):
        def spread(at, t):
            return (nsec - 1 - at) + (steps - 1 - t)

        def columns(act, t, kind, ds, to, recv):
            for dc in (-1, 1):
                @pl.when(there(0, dc))
                def _(dc=dc):
                    copy = column_copy(t, kind, ds, dc, to, recv)
                    copy.start() if act == "start" else copy.wait_send()

        def column_waits(t, to, recv):
            for dc in (-1, 1):
                @pl.when(there(0, dc))
                def _(dc=dc):
                    side = 0 if dc < 0 else 1
                    remote(to.at[t, side], to.at[t, side], send_sem.at[t, 0, side],
                           recv.at[t, side], 0, 0, dc).wait_recv()

        def frame_sends(act):
            for t in range(steps):
                for dr, dc in DIRS:
                    @pl.when(there(dr, dc))
                    def _(t=t, dr=dr, dc=dc):
                        copy = frame_copy(t, spread(0, t) + 1, dr, dc)
                        copy.start() if act == "start" else copy.wait_send()

        if s == 0:
            for t in range(steps):
                load_frame(t).wait()
                stage_columns(xc[t, PAD:PAD + rows], col_x.at[t])
            frame_sends("start")

        for t in range(steps):
            e = spread(s, t)
            first, last = PAD - e, PAD + rows + e
            if t > 0:
                column_waits(t - 1, he, hrecv)
                ends = [he[t - 1, k].astype(jnp.float32) for k in range(2)]
                assemble(hc, ends, t - 1, first - 1, last + 1, ah)
                span = pl.ds(first * cols, (last - first) * cols)
                acc[span] = jnp.dot(patches(ah, first, last - first), kernel_of(1),
                                    preferred_element_type=jnp.float32)
            if s == 0:
                for dr, dc in DIRS:
                    @pl.when(there(dr, dc))
                    def _(dr=dr, dc=dc):
                        frame_wait(t, e + 1, dr, dc)
                ends = [
                    jnp.concatenate([
                        fe[t, k].astype(jnp.float32)[rows - PAD:],
                        fe[t, k + 1].astype(jnp.float32),
                        fe[t, k + 2].astype(jnp.float32)[:PAD],
                    ], axis=0)
                    for k in (0, 3)
                ]
            else:
                for n, (r, count) in enumerate(pieces(first - 1, last + 1)):
                    block_copy(t, n, r, count, -1).wait_recv()
                column_waits(t, xe, xrecv)
                ends = [xe[t, k].astype(jnp.float32) for k in range(2)]
            assemble(xc, ends, t, first - 1, last + 1, ax)
            if t == 0:
                load_w.wait()
            for n, (r, count) in enumerate(pieces(first, last)):
                part = pl.ds(r * cols, count * cols)
                pre = jnp.dot(patches(ax, r, count), kernel_of(0), preferred_element_type=jnp.float32)
                pre = pre + bias[...]
                if t > 0:
                    pre = pre + acc[part]
                cell = sigmoid(pre[:, :width]) * jnp.tanh(pre[:, 2 * width:3 * width])
                if t > 0:
                    cell = sigmoid(pre[:, width:2 * width]) * cell_mem[part] + cell
                hidden = sigmoid(pre[:, 3 * width:]) * jnp.tanh(cell)
                hidden = hidden.reshape(count, cols, width)
                above, below = max(0, PAD - r), max(0, r + count - PAD - rows)
                if above or below:
                    bands = [hidden[:above] * top, hidden[above:count - below], hidden[count - below:] * bottom]
                    hidden = jnp.concatenate([b for b in bands if b.shape[0]], axis=0)
                hidden = hidden.astype(jnp.bfloat16)
                if t < steps - 1:
                    cell_mem[part] = cell
                    hc[t, pl.ds(r, count)] = hidden
                else:
                    if s < nsec - 1:
                        hc[t, pl.ds(r, count)] = hidden
                    low, up = max(r, PAD), min(r + count, PAD + rows)
                    if low < up:
                        cell_out[0, low - PAD:up - PAD] = cell.reshape(count, cols, width)[low - r:up - r]
                        hid_out[0, low - PAD:up - PAD] = hidden[low - r:up - r]
                if s < nsec - 1:
                    block_copy(t, n, r, count, 1).start()
            if t < steps - 1 or s < nsec - 1:
                stage_columns(hc[t], col_h.at[t])
            if t < steps - 1:
                columns("start", t, 0, 0, he, hrecv)
            if s < nsec - 1:
                columns("start", t, 1, 1, xe, xrecv)

        if s == 0:
            frame_sends("wait")
        for t in range(steps):
            if t < steps - 1:
                columns("wait", t, 0, 0, he, hrecv)
            if s < nsec - 1:
                columns("wait", t, 1, 1, xe, xrecv)
                e = spread(s, t)
                for n, (r, count) in enumerate(pieces(PAD - e, PAD + rows + e)):
                    block_copy(t, n, r, count, 1).wait_send()

    for s in range(nsec):
        @pl.when(sec == s)
        def _(s=s):
            section(s)


def solution(mesh):
    sizes = (mesh.shape["section"], mesh.shape["row"], mesh.shape["col"])

    def step(frames, weight, bias):
        steps, rows, cols, width = frames.shape
        high = rows + 2 * PAD
        vmem = pl.BlockSpec(memory_space=pltpu.VMEM)
        hbm = pl.BlockSpec(memory_space=pl.ANY)
        bf16 = jnp.bfloat16
        return pl.pallas_call(
            lambda *refs: body(sizes, *refs),
            out_shape=(
                jax.ShapeDtypeStruct((1, rows, cols, width), bf16),
                jax.ShapeDtypeStruct((1, rows, cols, width), jnp.float32),
            ),
            in_specs=[hbm, hbm, vmem],
            out_specs=(vmem, vmem),
            scratch_shapes=[
                pltpu.VMEM((steps, high, cols, width), bf16),
                pltpu.VMEM((steps, 2, high, width), bf16),
                pltpu.VMEM((steps, 6, rows, width), bf16),
                pltpu.VMEM((steps, high, cols, width), bf16),
                pltpu.VMEM((steps, 2, high, width), bf16),
                pltpu.VMEM((steps, 2, rows, width), bf16),
                pltpu.VMEM((steps, 2, high, width), bf16),
                pltpu.VMEM(weight.shape[1:], bf16),
                pltpu.VMEM((high, cols, 3 * width), bf16),
                pltpu.VMEM((high, cols, 3 * width), bf16),
                pltpu.VMEM((high * cols, 4 * width), jnp.float32),
                pltpu.VMEM((high * cols, width), jnp.float32),
                pltpu.SemaphoreType.DMA((steps + 1,)),
                pltpu.SemaphoreType.DMA((steps, 3, 9)),
                pltpu.SemaphoreType.DMA((steps, 9)),
                pltpu.SemaphoreType.DMA((steps, 9)),
                pltpu.SemaphoreType.DMA((steps, 2)),
            ],
            compiler_params=pltpu.CompilerParams(collective_id=0, has_side_effects=True),
        )(frames, weight, bias)

    return jax.shard_map(
        step,
        mesh=mesh,
        in_specs=(P(None, "row", "col", None), P("section", None, None, None), P("section", None)),
        out_specs=(P("section", "row", "col", None), P("section", "row", "col", None)),
        check_vma=False,
    )
```

time: 158 us -> 39 us (0.25)
  the two profiles are of different devices: /device:TPU:2 before, /device:TPU:3 now
where the time goes in v2:
time: 39 us; the launch traced here: 38.9 us
  Pallas kernels  35 us (90%)
  local copies, waits for them, and re-layouts  3.24 us (8%)
  between operations  0.64 us (2%)
    pallas_call x1, Pallas kernels, step(): pl.pallas_call(lambda *refs: body(sizes, *refs), out_shape=(jax.ShapeDtyp...  35 us
    unnamed x2, local copies, waits for them, and re-layouts  3.24 us

profile of v2, /device:TPU:3, one launch (start us, length us, event | category | flops | bytes accessed | tf_op | source)
XLA Modules:
  0.0 38.9 jit_solution(10072569378366898636)
XLA Ops:
  0.6 35.0 %shard_map.50 = (bf16[1,16,32,128]{3,2,1,0:T(8,128)(2,1)}, f32[1,16,32,128]{3,2,1,0:T(8,128)}) custom-call(bf16[3,16,32,128]{3,2,1,0:T(8,128)(2,1)} %refs_0_.1, bf16[1,9,256,512]{3,2,1,0:T(8,128)(2,1)} %refs_1_.1, f32[1,512]{1,0:T(1,128)} %refs_2_.1), custom_call_target="tpu_custom_call" | custom-call | tf_op jit(solution)/shard_map/pallas_call | solution.py:272
  35.6 1.6 %copy.7 = bf16[1,16,32,128]{3,2,1,0:T(8,128)(2,1)} copy(bf16[1,16,32,128]{3,2,1,0:T(8,128)(2,1)} %get-tuple-element.4) | data formatting | bytes 262144
  37.2 1.7 %copy.8 = f32[1,16,32,128]{3,2,1,0:T(8,128)} copy(f32[1,16,32,128]{3,2,1,0:T(8,128)} %get-tuple-element.5) | data formatting | bytes 524288

commit v3 on v1

v3 whole, which is shorter than its diff:
```python
import jax
import jax.numpy as jnp
from jax import lax
from jax.experimental import pallas as pl
from jax.experimental.pallas import tpu as pltpu
from jax.sharding import PartitionSpec as P

MESH = pl.DeviceIdType.MESH
DIRS = [(dr, dc) for dr in (-1, 0, 1) for dc in (-1, 0, 1) if (dr, dc) != (0, 0)]
SIDE = 8
CHUNK = 6


def sigmoid(v):
    return 0.5 * jnp.tanh(0.5 * v) + 0.5


def slot(dr, dc):
    return (dr + 1) * 3 + (dc + 1)


def body(sizes, frames, weight, bias, hid_out, cell_out,
         xc, xe, hc, col_x, col_h, w, ax, ah, acc, cell_mem,
         local_sem, send_sem, xrecv):
    nsec, nrow, ncol = sizes
    steps, rows, cols, width = frames.shape
    pad = steps
    wide = cols + 2 * SIDE
    sec, row, col = lax.axis_index("section"), lax.axis_index("row"), lax.axis_index("col")

    def load_frame(t):
        return pltpu.make_async_copy(frames.at[t], xc.at[t, pl.ds(pad, rows)], local_sem.at[t])

    load_w = pltpu.make_async_copy(weight.at[0], w, local_sem.at[steps])

    @pl.when(sec == 0)
    def _():
        for t in range(steps):
            load_frame(t).start()

    load_w.start()

    def there(dr, dc):
        ok = sec >= 0
        if dr:
            ok = (row > 0) if dr < 0 else (row < nrow - 1)
        if dc:
            okc = (col > 0) if dc < 0 else (col < ncol - 1)
            ok = jnp.logical_and(ok, okc) if dr else okc
        return ok

    def device(ds, dr, dc):
        return {"section": sec + ds, "row": row + dr, "col": col + dc}

    barrier = pltpu.get_barrier_semaphore()

    for t in range(steps):
        xc[t, 0:pad] = jnp.zeros((pad, cols, width), jnp.bfloat16)
        xc[t, pad + rows:] = jnp.zeros((pad, cols, width), jnp.bfloat16)
        xe[t] = jnp.zeros(xe.shape[1:], jnp.bfloat16)

    for ds in (-1, 0, 1):
        okd = (sec > 0) if ds < 0 else (sec < nsec - 1) if ds > 0 else (sec == 0)
        for dr, dc in [(0, 0)] + DIRS:
            if ds == 0 and (dr, dc) == (0, 0):
                continue

            @pl.when(jnp.logical_and(there(dr, dc), okd))
            def _(ds=ds, dr=dr, dc=dc):
                pl.semaphore_signal(barrier, inc=1, device_id=device(ds, dr, dc), device_id_type=MESH)

    def extent(pos, count):
        return 1 + jnp.where(pos > 0, 1, 0) + jnp.where(pos < count - 1, 1, 0)

    near = extent(row, nrow) * extent(col, ncol)
    pl.semaphore_wait(barrier, (extent(sec, nsec) - 1) * near + jnp.where(sec == 0, near - 1, 0))

    def halo_copy(center, base, colbuf, t, kind, ds, dr, dc):
        reach = steps - t
        if dr == 0:
            mine, theirs = pl.ds(0, rows), pl.ds(pad, rows)
        elif dr < 0:
            mine, theirs = pl.ds(0, reach), pl.ds(pad + rows, reach)
        else:
            mine, theirs = pl.ds(rows - reach, reach), pl.ds(pad - reach, reach)
        if dc == 0:
            src = center.at[t, pl.ds(base + (rows - reach if dr > 0 else 0), reach)]
            dst = xc.at[t, theirs]
        else:
            src = colbuf.at[t, 1 if dc > 0 else 0, mine]
            dst = xe.at[t, 0 if dc > 0 else 1, theirs]
        return pltpu.make_async_remote_copy(
            src_ref=src, dst_ref=dst,
            send_sem=send_sem.at[t, kind, slot(dr, dc)],
            recv_sem=xrecv.at[t, slot(-dr, -dc)],
            device_id=device(ds, dr, dc), device_id_type=MESH,
        )

    def halo_sends(act, center, base, colbuf, t, kind, ds):
        for dr, dc in sorted(DIRS, key=lambda d: -abs(d[0]) - abs(d[1])):
            @pl.when(there(dr, dc))
            def _(dr=dr, dc=dc):
                copy = halo_copy(center, base, colbuf, t, kind, ds, dr, dc)
                copy.start() if act == "start" else copy.wait_send()

    def halo_waits(t):
        reach = steps - t
        for dr, dc in DIRS:
            @pl.when(there(dr, dc))
            def _(dr=dr, dc=dc):
                mine = pl.ds(pad, rows) if dr == 0 else pl.ds(pad - reach if dr < 0 else pad + rows, reach)
                dst = xc.at[t, mine] if dc == 0 else xe.at[t, 0 if dc < 0 else 1, mine]
                pltpu.make_async_remote_copy(
                    src_ref=dst, dst_ref=dst,
                    send_sem=send_sem.at[t, 0, slot(0, 0)],
                    recv_sem=xrecv.at[t, slot(dr, dc)],
                    device_id=device(0, dr, dc), device_id_type=MESH,
                ).wait_recv()

    def center_copy(t):
        return pltpu.make_async_remote_copy(
            src_ref=hc.at[t], dst_ref=xc.at[t, pl.ds(pad, rows)],
            send_sem=send_sem.at[t, 0, slot(0, 0)], recv_sem=xrecv.at[t, slot(0, 0)],
            device_id=device(1, 0, 0), device_id_type=MESH,
        )

    @pl.when(sec == 0)
    def _():
        for t in range(steps):
            load_frame(t).wait()
            value = xc[t, pad:pad + rows].astype(jnp.float32)
            col_x[t, 0] = value[:, :SIDE].astype(jnp.bfloat16)
            col_x[t, 1] = value[:, cols - SIDE:].astype(jnp.bfloat16)
            halo_sends("start", xc, pad, col_x, t, 1, 0)

    place = lax.broadcasted_iota(jnp.int32, (wide, width), 0)
    left = jnp.where(col > 0, 1.0, 0.0)
    right = jnp.where(col < ncol - 1, 1.0, 0.0)
    inside = jnp.where(place < SIDE, left, jnp.where(place >= SIDE + cols, right, 1.0))
    above = jnp.where(row > 0, 1.0, 0.0)
    below = jnp.where(row < nrow - 1, 1.0, 0.0)

    def put(out, r, line, full):
        shifted = [pltpu.roll(line, 1, 0), line, pltpu.roll(line, wide - 1, 0)]
        for k, v in enumerate(shifted):
            v = v if full else v[SIDE:SIDE + cols]
            out[r, 0:v.shape[0], k * width:(k + 1) * width] = v.astype(jnp.bfloat16)

    def patches(a, first, count, span):
        return jnp.concatenate(
            [a[first + k:first + k + count, 0:span].reshape(count * span, 3 * width) for k in (-1, 0, 1)], axis=-1
        )

    def kernel_of(half):
        return w[:, half * width:(half + 1) * width, :].reshape(9 * width, 4 * width)

    for t in range(steps):
        e = steps - 1 - t
        full = t < steps - 1
        span = wide if full else cols
        first, last = pad - e, pad + rows + e
        total = (last - first) * span
        if t > 0:
            acc[0:total] = jnp.dot(patches(ah, first, last - first, span), kernel_of(1),
                                   preferred_element_type=jnp.float32)

        @pl.when(sec > 0)
        def _(t=t):
            center = xc.at[t, pl.ds(pad, rows)]
            pltpu.make_async_remote_copy(
                src_ref=center, dst_ref=center, send_sem=send_sem.at[t, 0, slot(0, 0)],
                recv_sem=xrecv.at[t, slot(0, 0)], device_id=device(-1, 0, 0), device_id_type=MESH,
            ).wait_recv()

        halo_waits(t)
        for r in range(first - 1, last + 1):
            line = jnp.concatenate([v.astype(jnp.float32) for v in (xe[t, 0, r], xc[t, r], xe[t, 1, r])], axis=0)
            put(ax, r, line, full)
        if t == 0:
            load_w.wait()
        for r in range(first, last, CHUNK):
            count = min(CHUNK, last - r)
            at = (r - first) * span
            pre = jnp.dot(patches(ax, r, count, span), kernel_of(0), preferred_element_type=jnp.float32)
            pre = pre + bias[...]
            if t > 0:
                pre = pre + acc[at:at + count * span]
            cell = sigmoid(pre[:, :width]) * jnp.tanh(pre[:, 2 * width:3 * width])
            cell = cell.reshape(count, span, width)
            if t > 0:
                old = cell_mem[r:r + count]
                old = old if full else old[:, SIDE:SIDE + cols]
                cell = sigmoid(pre[:, width:2 * width]).reshape(count, span, width) * old + cell
            hidden = sigmoid(pre[:, 3 * width:]).reshape(count, span, width) * jnp.tanh(cell)
            if full:
                cell_mem[r:r + count] = cell
            else:
                cell_out[0, r - pad:r - pad + count] = cell
                hid_out[0, r - pad:r - pad + count] = hidden.astype(jnp.bfloat16)
            for q in range(r, r + count):
                line = hidden[q - r]
                core = line[SIDE:SIDE + cols] if full else line
                if pad <= q < pad + rows:
                    hc[t, q - pad] = core.astype(jnp.bfloat16)
                    col_h[t, 0, q - pad] = core[:SIDE].astype(jnp.bfloat16)
                    col_h[t, 1, q - pad] = core[cols - SIDE:].astype(jnp.bfloat16)
                if full:
                    line = line * inside
                    line = line * above if q < pad else line * below if q >= pad + rows else line
                    put(ah, q, line, t + 1 < steps - 1)

        @pl.when(sec < nsec - 1)
        def _(t=t):
            halo_sends("start", hc, 0, col_h, t, 0, 1)
            center_copy(t).start()

    @pl.when(sec == 0)
    def _():
        for t in range(steps):
            halo_sends("wait", xc, pad, col_x, t, 1, 0)

    @pl.when(sec < nsec - 1)
    def _():
        for t in range(steps):
            center_copy(t).wait_send()
            halo_sends("wait", hc, 0, col_h, t, 0, 1)


def solution(mesh):
    sizes = (mesh.shape["section"], mesh.shape["row"], mesh.shape["col"])

    def step(frames, weight, bias):
        steps, rows, cols, width = frames.shape
        high, wide = rows + 2 * steps, cols + 2 * SIDE
        vmem = pl.BlockSpec(memory_space=pltpu.VMEM)
        hbm = pl.BlockSpec(memory_space=pl.ANY)
        bf16 = jnp.bfloat16
        return pl.pallas_call(
            lambda *refs: body(sizes, *refs),
            out_shape=(
                jax.ShapeDtypeStruct((1, rows, cols, width), bf16),
                jax.ShapeDtypeStruct((1, rows, cols, width), jnp.float32),
            ),
            in_specs=[hbm, hbm, vmem],
            out_specs=(vmem, vmem),
            scratch_shapes=[
                pltpu.VMEM((steps, high, cols, width), bf16),
                pltpu.VMEM((steps, 2, high, SIDE, width), bf16),
                pltpu.VMEM((steps, rows, cols, width), bf16),
                pltpu.VMEM((steps, 2, rows, SIDE, width), bf16),
                pltpu.VMEM((steps, 2, rows, SIDE, width), bf16),
                pltpu.VMEM(weight.shape[1:], bf16),
                pltpu.VMEM((high, wide, 3 * width), bf16),
                pltpu.VMEM((high, wide, 3 * width), bf16),
                pltpu.VMEM((high * wide, 4 * width), jnp.float32),
                pltpu.VMEM((high, wide, width), jnp.float32),
                pltpu.SemaphoreType.DMA((steps + 1,)),
                pltpu.SemaphoreType.DMA((steps, 2, 9)),
                pltpu.SemaphoreType.DMA((steps, 9)),
            ],
            compiler_params=pltpu.CompilerParams(collective_id=0, has_side_effects=True),
        )(frames, weight, bias)

    return jax.shard_map(
        step,
        mesh=mesh,
        in_specs=(P(None, "row", "col", None), P("section", None, None, None), P("section", None)),
        out_specs=(P("section", "row", "col", None), P("section", "row", "col", None)),
        check_vma=False,
    )
```

time: 36.8 us -> 34.3 us (0.932)
  Pallas kernels: 32.8 us -> 30.2 us
    pallas_call x1, Pallas kernels: 32.8 us -> 30.2 us  [step(): pl.pallas_call(lambda *refs: body(sizes, *refs), out_shape=(jax.ShapeDtyp...]
where the time goes in v3:
time: 34.3 us; the launch traced here: 34.1 us
  Pallas kernels  30.2 us (88%)
  local copies, waits for them, and re-layouts  3.24 us (9%)
  between operations  0.64 us (2%)
    pallas_call x1, Pallas kernels, step(): pl.pallas_call(lambda *refs: body(sizes, *refs), out_shape=(jax.ShapeDtyp...  30.2 us
    unnamed x2, local copies, waits for them, and re-layouts  3.24 us

profile of v3, /device:TPU:3, one launch (start us, length us, event | category | flops | bytes accessed | tf_op | source)
XLA Modules:
  0.0 34.1 jit_solution(13650664736827990328)
XLA Ops:
  0.6 30.2 %shard_map.50 = (bf16[1,16,32,128]{3,2,1,0:T(8,128)(2,1)}, f32[1,16,32,128]{3,2,1,0:T(8,128)}) custom-call(bf16[3,16,32,128]{3,2,1,0:T(8,128)(2,1)} %refs_0_.1, bf16[1,9,256,512]{3,2,1,0:T(8,128)(2,1)} %refs_1_.1, f32[1,512]{1,0:T(1,128)} %refs_2_.1), custom_call_target="tpu_custom_call" | custom-call | tf_op jit(solution)/shard_map/pallas_call | solution.py:238
  30.9 1.6 %copy.7 = bf16[1,16,32,128]{3,2,1,0:T(8,128)(2,1)} copy(bf16[1,16,32,128]{3,2,1,0:T(8,128)(2,1)} %get-tuple-element.4) | data formatting | bytes 262144
  32.4 1.7 %copy.8 = f32[1,16,32,128]{3,2,1,0:T(8,128)} copy(f32[1,16,32,128]{3,2,1,0:T(8,128)} %get-tuple-element.5) | data formatting | bytes 524288

commit v4 on v3

--- a/solution.py
+++ b/solution.py
@@ -19,7 +19,7 @@
     return (dr + 1) * 3 + (dc + 1)
 
 
-def body(sizes, frames, weight, bias, hid_out, cell_out,
+def body(sizes, frames, weight, bias, kept_out, added_out, gate_out,
          xc, xe, hc, col_x, col_h, w, ax, ah, acc, cell_mem,
          local_sem, send_sem, xrecv):
     nsec, nrow, ncol = sizes
@@ -185,18 +185,22 @@
             pre = pre + bias[...]
             if t > 0:
                 pre = pre + acc[at:at + count * span]
-            cell = sigmoid(pre[:, :width]) * jnp.tanh(pre[:, 2 * width:3 * width])
-            cell = cell.reshape(count, span, width)
+            added = sigmoid(pre[:, :width]) * jnp.tanh(pre[:, 2 * width:3 * width])
+            added = added.reshape(count, span, width)
+            cell = added
             if t > 0:
                 old = cell_mem[r:r + count]
                 old = old if full else old[:, SIDE:SIDE + cols]
-                cell = sigmoid(pre[:, width:2 * width]).reshape(count, span, width) * old + cell
-            hidden = sigmoid(pre[:, 3 * width:]).reshape(count, span, width) * jnp.tanh(cell)
+                kept = sigmoid(pre[:, width:2 * width]).reshape(count, span, width) * old
+                cell = kept + added
+            opened = sigmoid(pre[:, 3 * width:]).reshape(count, span, width)
+            hidden = opened * jnp.tanh(cell)
             if full:
                 cell_mem[r:r + count] = cell
             else:
-                cell_out[0, r - pad:r - pad + count] = cell
-                hid_out[0, r - pad:r - pad + count] = hidden.astype(jnp.bfloat16)
+                kept_out[0, r - pad:r - pad + count] = kept
+                added_out[0, r - pad:r - pad + count] = added
+                gate_out[0, r - pad:r - pad + count] = opened
             for q in range(r, r + count):
                 line = hidden[q - r]
                 core = line[SIDE:SIDE + cols] if full else line
@@ -235,14 +239,11 @@
         vmem = pl.BlockSpec(memory_space=pltpu.VMEM)
         hbm = pl.BlockSpec(memory_space=pl.ANY)
         bf16 = jnp.bfloat16
-        return pl.pallas_call(
+        kept, added, opened = pl.pallas_call(
             lambda *refs: body(sizes, *refs),
-            out_shape=(
-                jax.ShapeDtypeStruct((1, rows, cols, width), bf16),
-                jax.ShapeDtypeStruct((1, rows, cols, width), jnp.float32),
-            ),
+            out_shape=(jax.ShapeDtypeStruct((1, rows, cols, width), jnp.float32),) * 3,
             in_specs=[hbm, hbm, vmem],
-            out_specs=(vmem, vmem),
+            out_specs=(vmem, vmem, vmem),
             scratch_shapes=[
                 pltpu.VMEM((steps, high, cols, width), bf16),
                 pltpu.VMEM((steps, 2, high, SIDE, width), bf16),
@@ -260,6 +261,8 @@
             ],
             compiler_params=pltpu.CompilerParams(collective_id=0, has_side_effects=True),
         )(frames, weight, bias)
+        cell = kept + added
+        return (opened * jnp.tanh(cell)).astype(bf16), cell
 
     return jax.shard_map(
         step,

time: 34.3 us -> 33.1 us (0.965)
  local copies, waits for them, and re-layouts: 3.24 us -> 0 us
  other arithmetic: 0 us -> 1.91 us
    unnamed x2 -> x0, local copies, waits for them, and re-layouts: 3.24 us -> none
    convert_element_type x0 -> x1, other arithmetic: none -> 1.91 us  [step(): return ((opened * jnp.tanh(cell)).astype(bf16), cell)]
where the time goes in v4:
time: 33.1 us; the launch traced here: 32.9 us
  Pallas kernels  30.4 us (92%)
  other arithmetic  1.91 us (6%)
  between operations  0.64 us (2%)
    pallas_call x1, Pallas kernels, step(): pl.pallas_call(lambda *refs: body(sizes, *refs), out_shape=(jax.ShapeDtyp...  30.4 us
    convert_element_type x1, other arithmetic, step(): return ((opened * jnp.tanh(cell)).astype(bf16), cell)  1.91 us

profile of v4, /device:TPU:3, one launch (start us, length us, event | category | flops | bytes accessed | tf_op | source)
XLA Modules:
  0.0 32.9 jit_solution(12533277966527583710)
XLA Ops:
  0.6 30.4 %shard_map.50 = (f32[1,16,32,128]{3,2,1,0:T(8,128)}, f32[1,16,32,128]{3,2,1,0:T(8,128)}, f32[1,16,32,128]{3,2,1,0:T(8,128)}) custom-call(bf16[3,16,32,128]{3,2,1,0:T(8,128)(2,1)} %refs_0_.1, bf16[1,9,256,512]{3,2,1,0:T(8,128)(2,1)} %refs_1_.1, f32[1,512]{1,0:T(1,128)} %refs_2_.1), custom_call_target="tpu_custom_call" | custom-call | tf_op jit(solution)/shard_map/pallas_call | solution.py:242
  31.0 1.9 %multiply_convert_fusion = (bf16[1,16,32,128]{3,2,1,0:T(8,128)(2,1)}, f32[1,16,32,128]{3,2,1,0:T(8,128)}) fusion(f32[1,16,32,128]{3,2,1,0:T(8,128)} %get-tuple-element.5, f32[1,16,32,128]{3,2,1,0:T(8,128)} %get-tuple-element.6, f32[1,16,32,128]{3,2,1,0:T(8,128)} %get-tuple-element.7), kind=kLoop, calls=%fused_computation | loop fusion | flops 196608 | bytes 1179648 | tf_op jit(solution)/shard_map/convert_element_type | solution.py:265
